TPU v7x, 256 devices: a whole 4x4x8 slice. The times are simulated.
256 devices in a mesh: seq: 128 (over y, x_lo, z, core), tp: 2 (over x_hi).
Axes of the slice: x: 4 (x_hi: 2, x_lo: 2; x = x_hi * 2 + x_lo), y: 4, z: 8, core: 2. Of those that a mesh axis runs over, the one named last changes fastest.
Arguments:
- series: bfloat16 [32768, 2048], P(('seq', 'tp')), may hold values from -4 to 4
- norm_gain: float32 [2048], replicated, may hold values from 0.1 to 1.9
- w_query: bfloat16 [2048, 1024], P(None, 'tp'), may hold values from -0.5 to 0.5
- w_key: bfloat16 [2048, 1024], P(None, 'tp'), may hold values from -0.5 to 0.5
- w_value: bfloat16 [2048, 1024], P(None, 'tp'), may hold values from -0.125 to 0.125
- w_out: bfloat16 [1024, 2048], P('tp'), may hold values from -0.1875 to 0.1875
- out_grad: bfloat16 [32768, 2048], P(('seq', 'tp')), may hold values from -6 to 6
Outputs:
- layer_out: bfloat16 [32768, 2048], P(('seq', 'tp'))
- series_grad: bfloat16 [32768, 2048], P(('seq', 'tp'))
All inputs are finite; a program needn't handle non-finite values.
Results may differ from a plain program's by a relative error of at most 0.019.
Values may be sent and summed in bfloat16 or wider, within the bound.
No kernel may reach another device: no remote copies, remote signals or barrier semaphores. Data moves between devices by JAX's collectives and lax.ppermute only.
A program may use at most 128 MiB of HBM per device.

v0:
```python
import jax
import jax.numpy as jnp
from jax import lax
from jax.sharding import PartitionSpec as P

HD = 128
BLOCK = 64
NEG = -1e30
EPS = 1e-06


def shifted(value, axis, by):
    size = lax.axis_size(axis)
    pairs = [(i, i + by) for i in range(size) if 0 <= i + by < size]
    return lax.ppermute(value, axis, pairs)


def project_back(grads, weight):
    return jnp.einsum("tf,df->td", grads, weight, preferred_element_type=jnp.float32)


def per_device(series, norm_gain, w_query, w_key, w_value, w_out, out_grad):
    series_f = series.astype(jnp.float32)
    inv_rms = lax.rsqrt(jnp.mean(series_f * series_f, axis=-1, keepdims=True) + EPS)
    unit_rows = series_f * inv_rms
    normed_rows = (unit_rows * norm_gain).astype(jnp.bfloat16)
    gathered, out_grads = (
        lax.all_gather(normed_rows, "tp", axis=0, tiled=True),
        lax.all_gather(out_grad, "tp", axis=0, tiled=True),
    )
    tokens = gathered.shape[0]
    feat_width = w_query.shape[1]
    head_count = feat_width // HD
    blocks = tokens // BLOCK
    seq_devices = lax.axis_size("seq")
    levels = seq_devices.bit_length() - 1
    first_block = lax.axis_index("seq") * blocks
    factor = HD ** (-0.5)
    query_rows = jnp.dot(gathered, w_query, preferred_element_type=jnp.float32).astype(jnp.bfloat16)
    key_rows = jnp.dot(gathered, w_key, preferred_element_type=jnp.float32).astype(jnp.bfloat16)
    value_rows = jnp.dot(gathered, w_value, preferred_element_type=jnp.float32).astype(jnp.bfloat16)
    key_value = jnp.stack([key_rows, value_rows])
    fetched = [shifted(key_value, "seq", 2**section) for section in range(levels)]
    near_steps = [2**section for section in range(blocks.bit_length())]
    distances = near_steps + [blocks * 2**section for section in range(1, levels)]
    own_blocks = key_value.reshape(2, blocks, BLOCK, feat_width)
    extended = jnp.concatenate([fetched[0], key_value], axis=1).reshape(
        2, 2 * blocks, BLOCK, feat_width
    )
    pieces = [own_blocks] + [
        extended[:, blocks - distance : 2 * blocks - distance] for distance in near_steps
    ]
    pieces = pieces + [
        fetched[section].reshape(2, blocks, BLOCK, feat_width) for section in range(1, levels)
    ]
    keys_all = jnp.concatenate(pieces, axis=2)
    global_block = first_block + jnp.arange(blocks, dtype=jnp.int32)
    causal = lax.broadcasted_iota(jnp.int32, (BLOCK, BLOCK), 0) >= lax.broadcasted_iota(
        jnp.int32, (BLOCK, BLOCK), 1
    )
    mask_list = [jnp.broadcast_to(causal, (blocks, BLOCK, BLOCK))]
    mask_list = mask_list + [
        jnp.broadcast_to((global_block >= distance)[:, None, None], (blocks, BLOCK, BLOCK))
        for distance in distances
    ]
    key_mask = jnp.concatenate(mask_list, axis=2)[:, None]
    query_blocks = query_rows.reshape(blocks, BLOCK, head_count, HD)
    key_blocks = keys_all[0].reshape(blocks, -1, head_count, HD)
    value_blocks = keys_all[1].reshape(blocks, -1, head_count, HD)
    scores = (
        jnp.einsum("bqhe,bkhe->bhqk", query_blocks, key_blocks, preferred_element_type=jnp.float32)
        * factor
    )
    scores = jnp.where(key_mask, scores, NEG)
    peak_score = jnp.max(scores, axis=-1, keepdims=True)
    log_total = peak_score + jnp.log(jnp.sum(jnp.exp(scores - peak_score), axis=-1, keepdims=True))
    attn_prob = jnp.exp(scores - log_total)
    attn_weight = attn_prob.astype(jnp.bfloat16)
    mixed = jnp.einsum(
        "bhqk,bkhe->bqhe", attn_weight, value_blocks, preferred_element_type=jnp.float32
    ).astype(jnp.bfloat16)
    mixed_rows = mixed.reshape(tokens, feat_width)
    attn_rows = lax.psum_scatter(
        jnp.dot(mixed_rows, w_out, preferred_element_type=jnp.float32).astype(jnp.bfloat16),
        "tp",
        scatter_dimension=0,
        tiled=True,
    ).astype(jnp.float32)
    layer_out = (series_f + attn_rows).astype(jnp.bfloat16)
    grad_mixed = jnp.einsum(
        "td,fd->tf", out_grads, w_out, preferred_element_type=jnp.float32
    ).astype(jnp.bfloat16)
    grad_blocks = grad_mixed.reshape(blocks, BLOCK, head_count, HD)
    row_inner = jnp.einsum("bqhe,bqhe->bhq", grad_blocks, mixed, preferred_element_type=jnp.float32)
    grad_probs = jnp.einsum(
        "bqhe,bkhe->bhqk", grad_blocks, value_blocks, preferred_element_type=jnp.float32
    )
    grad_scores = (attn_prob * (grad_probs - row_inner[..., None])).astype(jnp.bfloat16)
    grad_query = (
        jnp.einsum("bhqk,bkhe->bqhe", grad_scores, key_blocks, preferred_element_type=jnp.float32)
        * factor
    ).astype(jnp.bfloat16)
    grad_query = grad_query.reshape(tokens, feat_width)
    grad_keys = (
        jnp.einsum("bhqk,bqhe->bkhe", grad_scores, query_blocks, preferred_element_type=jnp.float32)
        * factor
    )
    grad_values = jnp.einsum(
        "bhqk,bqhe->bkhe", attn_weight, grad_blocks, preferred_element_type=jnp.float32
    )
    grad_pairs = jnp.stack([grad_keys, grad_values]).reshape(2, blocks, -1, BLOCK, feat_width)
    spill_grads = jnp.zeros((2, 2 * blocks, BLOCK, feat_width), jnp.float32)
    for position, distance in enumerate(near_steps):
        spill_grads = spill_grads.at[:, blocks - distance : 2 * blocks - distance].add(
            grad_pairs[:, :, 1 + position]
        )
    own_grads = grad_pairs[:, :, 0] + spill_grads[:, blocks:]
    for section in range(levels):
        if section == 0:
            return_part = spill_grads[:, :blocks]
        else:
            return_part = grad_pairs[:, :, len(near_steps) + section]
        own_grads = own_grads + shifted(return_part, "seq", -(2**section))
    grad_key_rows = own_grads[0].reshape(tokens, feat_width).astype(jnp.bfloat16)
    grad_value_rows = own_grads[1].reshape(tokens, feat_width).astype(jnp.bfloat16)
    grad_normed = (
        project_back(grad_query, w_query)
        + project_back(grad_key_rows, w_key)
        + project_back(grad_value_rows, w_value)
    )
    grad_own = lax.psum_scatter(
        grad_normed.astype(jnp.bfloat16), "tp", scatter_dimension=0, tiled=True
    ).astype(jnp.float32)
    scaled = grad_own * norm_gain
    series_grad = out_grad.astype(jnp.float32) + inv_rms * (
        scaled - unit_rows * jnp.mean(scaled * unit_rows, axis=-1, keepdims=True)
    )
    return (layer_out, series_grad.astype(jnp.bfloat16))


def solution(mesh):
    in_specs = (
        P(("seq", "tp"), None),
        P(),
        P(None, "tp"),
        P(None, "tp"),
        P(None, "tp"),
        P("tp", None),
        P(("seq", "tp"), None),
    )
    out_specs = (P(("seq", "tp"), None), P(("seq", "tp"), None))
    return jax.shard_map(
        per_device, mesh=mesh, in_specs=in_specs, out_specs=out_specs, check_vma=False
    )
```

profile of v0, /device:TPU:1, one launch (start us, length us, event | category | flops | bytes accessed | tf_op | source)
XLA Modules:
  0.0 416.9 jit_solution(14355555327161746175)
XLA Ops:
  13.3 29.2 %all-gather.3.cloned.1.call-done = bf16[256,2048]{1,0:T(8,128)(2,1)} async-done(((bf16[128,2048]{1,0:T(8,128)(2,1)}), bf16[256,2048]{1,0:T(8,128)(2,1)}) %all-gather.3.cloned.1.call-update) | async-done | bytes 1048592 | tf_op jit(solution)/shard_map/all_gather | solution.py:28
  42.5 2.8 convolution_convert_fusion.4
  46.9 3.7 collective-permute-start
  50.6 3.2 collective-permute-start.1
  53.8 6.2 %collective-permute-start.2 = (bf16[2,256,512]{2,1,0:T(8,128)(2,1)}, bf16[2,256,512]{2,1,0:T(8,128)(2,1)}, u32[]{:S(2)}, u32[]{:S(2)}) collective-permute-start(bf16[2,256,512]{2,1,0:T(8,128)(2,1)} %pad_maximum_fusion.1), channel_id=1, source_target_pairs={{0,8},{2,10},{4,12},{6,14},{8,16},{10,18},{12,20},{14,22},{16,24},... | collective-permute-start | bytes 1572872 | tf_op jit(solution)/shard_map/ppermute | solution.py:15
  62.2 3.7 collective-permute-start.4
  70.6 46.3 %all-gather.5.cloned.1.call-done = bf16[256,2048]{1,0:T(8,128)(2,1)} async-done(((bf16[128,2048]{1,0:T(8,128)(2,1)}), bf16[256,2048]{1,0:T(8,128)(2,1)}) %all-gather.5.cloned.1.call-update) | async-done | bytes 1048592 | tf_op jit(solution)/shard_map/all_gather | solution.py:29
  116.9 2.7 convolution_convert_fusion.2
  120.5 3.9 collective-permute-start.5
  125.2 4.4 %collective-permute-start.6 = (bf16[2,256,512]{2,1,0:T(8,128)(2,1)}, bf16[2,256,512]{2,1,0:T(8,128)(2,1)}, u32[]{:S(2)}, u32[]{:S(2)}) collective-permute-start(bf16[2,256,512]{2,1,0:T(8,128)(2,1)} %pad_maximum_fusion.1), channel_id=1, source_target_pairs={{0,128},{2,130},{4,132},{6,134},{8,136},{10,138},{12,140},{14,142}... | collective-permute-start | bytes 1572872 | tf_op jit(solution)/shard_map/ppermute | solution.py:15
  138.0 2.5 copy.66
  147.6 2.4 copy.30
  154.8 12.3 %concatenate.18 = bf16[2,4,640,512]{2,3,1,0:T(8,128)(2,1)} concatenate(bf16[2,4,64,512]{2,3,1,0:T(8,128)(2,1)S(1)} %pad_maximum_fusion, bf16[2,4,64,512]{2,3,1,0:T(8,128)(2,1)} %copy.64, bf16[2,4,64,512]{2,3,1,0:T(8,128)(2,1)} %copy.65, bf16[2,4,64,512]{2,3,1,0:T(8,128)(2,1)} %copy.66, bf16[2,4,64,512]{2,3,1,0:T(8,128)(2,1)} %copy.27, bf16[2,4,64,512]{2,3,1,0:T(8,128)(2,1)} %copy.28, ...), dimensions={2} | concatenate | bytes 10485760 | tf_op jit(solution)/shard_map/concatenate | solution.py:56
  167.1 3.0 fusion.46
  172.5 3.2 convolution_bitcast_fusion
  178.5 3.3 multiply_bitcast_fusion
  181.8 7.2 %copy.42 = f32[4,640,4,128]{3,2,1,0:T(4,128)} copy(f32[4,640,4,128]{1,3,2,0:T(8,128)} %multiply_bitcast_fusion) | data formatting | bytes 10485760 | tf_op jit(solution)/shard_map/mul | solution.py:105
  189.0 7.4 %stack.30 = f32[1,4,10,64,512]{4,3,2,1,0:T(8,128)} reshape(f32[4,640,4,128]{3,2,1,0:T(4,128)} %copy.42) | data formatting | bytes 10485760 | tf_op jit(solution)/shard_map/stack | solution.py:111
  196.4 5.8 %constant_dynamic-update-slice_fusion.1 = f32[2,4,10,64,512]{4,3,2,1,0:T(8,128)} fusion(f32[1,4,10,64,512]{4,3,2,1,0:T(8,128)} %stack.30), kind=kLoop, calls=%fused_computation.73 | loop fusion | bytes 10485760
  202.2 7.2 %copy.44 = f32[4,640,4,128]{3,2,1,0:T(4,128)} copy(f32[4,640,4,128]{1,3,2,0:T(8,128)} %convolution_bitcast_fusion) | data formatting | bytes 10485760 | tf_op jit(solution)/shard_map/bhqk,bqhe->bkhe/transpose | solution.py:108
  209.4 7.4 %stack.31 = f32[1,4,10,64,512]{4,3,2,1,0:T(8,128)} reshape(f32[4,640,4,128]{3,2,1,0:T(4,128)} %copy.44) | data formatting | bytes 10485760 | tf_op jit(solution)/shard_map/stack | solution.py:111
  216.9 5.9 %constant_dynamic-update-slice_fusion = f32[2,4,10,64,512]{4,3,2,1,0:T(8,128)} fusion(f32[2,4,10,64,512]{4,3,2,1,0:T(8,128)} %constant_dynamic-update-slice_fusion.1, f32[1,4,10,64,512]{4,3,2,1,0:T(8,128)} %stack.31), kind=kLoop, calls=%fused_computation.72 | loop fusion | bytes 10485760 | tf_op jit(solution)/shard_map/stack | solution.py:111
  222.7 4.6 %slice_bitcast_fusion.8 = (f32[2,4,64,512]{3,2,1,0:T(8,128)S(1)}, f32[2,4,64,512]{3,2,1,0:T(8,128)S(1)}, f32[2,4,64,512]{3,2,1,0:T(8,128)S(1)}, f32[2,4,64,512]{...) fusion(f32[2,4,10,64,512]{4,3,2,1,0:T(8,128)} %constant_dynamic, ...), kind=kLoop, calls=%fused_computation.53 | loop fusion | bytes 14680064 | tf_op jit(solution)/shard_map/add | solution.py:114
  237.2 17.2 %collective-permute-done.13 = f32[2,4,64,512]{3,2,1,0:T(8,128)S(1)} collective-permute-done((f32[2,4,64,512]{3,2,1,0:T(8,128)S(1)}, f32[2,4,64,512]{3,2,1,0:T(8,128)S(1)}, u32[]{:S(2)}, u32[]{:S(2)}) %collective-permute-start.13) | collective-permute-done | bytes 1048608 | tf_op jit(solution)/shard_map/ppermute | solution.py:15
  255.7 4.1 collective-permute-start.7
  262.0 19.3 %collective-permute-done.9 = f32[2,4,64,512]{3,2,1,0:T(8,128)S(1)} collective-permute-done((f32[2,4,64,512]{3,2,1,0:T(8,128)S(1)}, f32[2,4,64,512]{3,2,1,0:T(8,128)S(1)}, u32[]{:S(2)}, u32[]{:S(2)}) %collective-permute-start.9) | collective-permute-done | bytes 1048608 | tf_op jit(solution)/shard_map/ppermute | solution.py:15
  281.3 21.0 %collective-permute-done.8 = f32[2,4,64,512]{3,2,1,0:T(8,128)S(1)} collective-permute-done((f32[2,4,64,512]{3,2,1,0:T(8,128)S(1)}, f32[2,4,64,512]{3,2,1,0:T(8,128)S(1)}, u32[]{:S(2)}, u32[]{:S(2)}) %collective-permute-start.8) | collective-permute-done | bytes 1048608 | tf_op jit(solution)/shard_map/ppermute | solution.py:15
  302.3 11.8 %collective-permute-done.7 = f32[2,4,64,512]{3,2,1,0:T(8,128)S(1)} collective-permute-done((f32[2,4,64,512]{3,2,1,0:T(8,128)S(1)}, f32[2,4,64,512]{3,2,1,0:T(8,128)S(1)}, u32[]{:S(2)}, u32[]{:S(2)}) %collective-permute-start.7) | collective-permute-done | bytes 1048608 | tf_op jit(solution)/shard_map/ppermute | solution.py:15
  320.0 3.3 convolution_convert_fusion
  323.4 55.4 %reduce-scatter.5.cloned.1.call-done = bf16[128,2048]{1,0:T(8,128)(2,1)} async-done(((bf16[256,2048]{1,0:T(8,128)(2,1)}), bf16[128,2048]{1,0:T(8,128)(2,1)}) %reduce-scatter.5.cloned.1.call-update) | async-done | bytes 524304 | tf_op jit(solution)/shard_map/reduce_scatter | solution.py:131
  380.2 27.5 %reduce-scatter.3.cloned.1.call-done = bf16[128,2048]{1,0:T(8,128)(2,1)} async-done(((bf16[256,2048]{1,0:T(8,128)(2,1)}), bf16[128,2048]{1,0:T(8,128)(2,1)}) %reduce-scatter.3.cloned.1.call-update) | async-done | bytes 524304 | tf_op jit(solution)/shard_map/reduce_scatter | solution.py:83
  407.7 2.7 fusion.12
  (123 shorter events, 62.0 us)
Async XLA Ops:
  7.2 60.7 %copy-start = (bf16[2048,512]{1,0:T(8,128)(2,1)S(1)}, bf16[2048,512]{1,0:T(8,128)(2,1)}, u32[]{:S(2)}) copy-start(bf16[2048,512]{1,0:T(8,128)(2,1)} %param.15) | copy-start | bytes 6291460
  7.2 35.3 %all-gather.3.cloned.1.call-start = ((), (), s32[]{:S(2)}) async-start(), calls=%async_computation.2 | async-start | bytes 1572864 | tf_op jit(solution)/shard_map/all_gather | solution.py:28
  10.7 106.2 %all-gather.5.cloned.1.call-start = ((), (), s32[]{:S(2)}) async-start(), calls=%async_computation.4 | async-start | bytes 1572864 | tf_op jit(solution)/shard_map/all_gather | solution.py:29
  11.4 367.4 %reduce-scatter.5.cloned.1.call-start = ((), (), s32[]{:S(2)}) async-start(), calls=%async_computation.5 | async-start | bytes 1572864 | tf_op jit(solution)/shard_map/reduce_scatter | solution.py:131
  45.3 21.6 %copy-start.7 = (bf16[256,512]{1,0:T(8,128)(2,1)}, bf16[256,512]{1,0:T(8,128)(2,1)S(1)}, u32[]{:S(2)}) copy-start(bf16[256,512]{1,0:T(8,128)(2,1)S(1)} %convolution_convert_fusion.4) | copy-start | bytes 786436
  46.0 23.8 %copy-start.9 = (bf16[256,512]{1,0:T(8,128)(2,1)}, bf16[256,512]{1,0:T(8,128)(2,1)S(1)}, u32[]{:S(2)}) copy-start(bf16[256,512]{1,0:T(8,128)(2,1)S(1)} %convolution_convert_fusion.5) | copy-start | bytes 786436
  46.9 73.6 %collective-permute-start = (bf16[2,256,512]{2,1,0:T(8,128)(2,1)}, bf16[2,256,512]{2,1,0:T(8,128)(2,1)}, u32[]{:S(2)}, u32[]{:S(2)}) collective-permute-start(bf16[2,256,512]{2,1,0:T(8,128)(2,1)} %pad_maximum_fusion.1), channel_id=1, source_target_pairs={{0,2},{2,4},{4,6},{6,8},{8,10},{10,12},{12,14},{14,16},{16,18},{18... | collective-permute-start | bytes 1572872 | tf_op jit(solution)/shard_map/ppermute | solution.py:15
  50.6 73.8 %collective-permute-start.1 = (bf16[2,256,512]{2,1,0:T(8,128)(2,1)}, bf16[2,256,512]{2,1,0:T(8,128)(2,1)S(1)}, u32[]{:S(2)}, u32[]{:S(2)}) collective-permute-start(bf16[2,256,512]{2,1,0:T(8,128)(2,1)} %pad_maximum_fusion.1), channel_id=1, source_target_pairs={{0,4},{2,6},{4,8},{6,10},{8,12},{10,14},{12,16},{14,18},{16,20},{1... | collective-permute-start | bytes 1572872 | tf_op jit(solution)/shard_map/ppermute | solution.py:15
  53.8 89.1 %collective-permute-start.2 = (bf16[2,256,512]{2,1,0:T(8,128)(2,1)}, bf16[2,256,512]{2,1,0:T(8,128)(2,1)}, u32[]{:S(2)}, u32[]{:S(2)}) collective-permute-start(bf16[2,256,512]{2,1,0:T(8,128)(2,1)} %pad_maximum_fusion.1), channel_id=1, source_target_pairs={{0,8},{2,10},{4,12},{6,14},{8,16},{10,18},{12,20},{14,22},{16,24},... | collective-permute-start | bytes 1572872 | tf_op jit(solution)/shard_map/ppermute | solution.py:15
  60.0 85.3 %collective-permute-start.3 = (bf16[2,256,512]{2,1,0:T(8,128)(2,1)}, bf16[2,256,512]{2,1,0:T(8,128)(2,1)}, u32[]{:S(2)}, u32[]{:S(2)}) collective-permute-start(bf16[2,256,512]{2,1,0:T(8,128)(2,1)} %pad_maximum_fusion.1), channel_id=1, source_target_pairs={{0,16},{2,18},{4,20},{6,22},{8,24},{10,26},{12,28},{14,30},{16,32}... | collective-permute-start | bytes 1572872 | tf_op jit(solution)/shard_map/ppermute | solution.py:15
  62.2 85.5 %collective-permute-start.4 = (bf16[2,256,512]{2,1,0:T(8,128)(2,1)}, bf16[2,256,512]{2,1,0:T(8,128)(2,1)}, u32[]{:S(2)}, u32[]{:S(2)}) collective-permute-start(bf16[2,256,512]{2,1,0:T(8,128)(2,1)} %pad_maximum_fusion.1), channel_id=1, source_target_pairs={{0,32},{2,34},{4,36},{6,38},{8,40},{10,42},{12,44},{14,46},{16,48}... | collective-permute-start | bytes 1572872 | tf_op jit(solution)/shard_map/ppermute | solution.py:15
  119.6 52.9 %copy-start.4 = (bf16[4,64,4,128]{3,2,1,0:T(4,128)(2,1)}, bf16[4,64,4,128]{3,2,1,0:T(4,128)(2,1)S(1)}, u32[]{:S(2)}) copy-start(bf16[4,64,4,128]{3,2,1,0:T(4,128)(2,1)S(1)} %reshape.218) | copy-start | bytes 786436
  119.6 11.4 %copy-start.8 = (bf16[256,512]{1,0:T(8,128)(2,1)S(1)}, bf16[256,512]{1,0:T(8,128)(2,1)}, u32[]{:S(2)}) copy-start(bf16[256,512]{1,0:T(8,128)(2,1)} %copy-done.7) | copy-start | bytes 786436
  119.6 11.4 %copy-start.10 = (bf16[256,512]{1,0:T(8,128)(2,1)S(1)}, bf16[256,512]{1,0:T(8,128)(2,1)}, u32[]{:S(2)}) copy-start(bf16[256,512]{1,0:T(8,128)(2,1)} %copy-done.9) | copy-start | bytes 786436
  120.5 29.6 %collective-permute-start.5 = (bf16[2,256,512]{2,1,0:T(8,128)(2,1)}, bf16[2,256,512]{2,1,0:T(8,128)(2,1)}, u32[]{:S(2)}, u32[]{:S(2)}) collective-permute-start(bf16[2,256,512]{2,1,0:T(8,128)(2,1)} %pad_maximum_fusion.1), channel_id=1, source_target_pairs={{0,64},{2,66},{4,68},{6,70},{8,72},{10,74},{12,76},{14,78},{16,80}... | collective-permute-start | bytes 1572872 | tf_op jit(solution)/shard_map/ppermute | solution.py:15
  125.2 27.2 %collective-permute-start.6 = (bf16[2,256,512]{2,1,0:T(8,128)(2,1)}, bf16[2,256,512]{2,1,0:T(8,128)(2,1)}, u32[]{:S(2)}, u32[]{:S(2)}) collective-permute-start(bf16[2,256,512]{2,1,0:T(8,128)(2,1)} %pad_maximum_fusion.1), channel_id=1, source_target_pairs={{0,128},{2,130},{4,132},{6,134},{8,136},{10,138},{12,140},{14,142}... | collective-permute-start | bytes 1572872 | tf_op jit(solution)/shard_map/ppermute | solution.py:15
  167.1 3.1 copy-start.6
  167.1 3.1 copy-start.17
  172.5 3.3 copy-start.13
  227.4 27.0 %collective-permute-start.13 = (f32[2,4,64,512]{3,2,1,0:T(8,128)S(1)}, f32[2,4,64,512]{3,2,1,0:T(8,128)S(1)}, u32[]{:S(2)}, u32[]{:S(2)}) collective-permute-start(f32[2,4,64,512]{3,2,1,0:T(8,128)S(1)} %get-tuple-element.43), channel_id=1, source_target_pairs={{128,0},{130,2},{132,4},{134,6},{136,8},{138,10},{140,12},{142,14}... | collective-permute-start | bytes 3145736 | tf_op jit(solution)/shard_map/ppermute | solution.py:15
  228.7 27.0 %collective-permute-start.12 = (f32[2,4,64,512]{3,2,1,0:T(8,128)S(1)}, f32[2,4,64,512]{3,2,1,0:T(8,128)S(1)}, u32[]{:S(2)}, u32[]{:S(2)}) collective-permute-start(f32[2,4,64,512]{3,2,1,0:T(8,128)S(1)} %get-tuple-element.44), channel_id=1, source_target_pairs={{64,0},{66,2},{68,4},{70,6},{72,8},{74,10},{76,12},{78,14},{80,16}... | collective-permute-start | bytes 3145736 | tf_op jit(solution)/shard_map/ppermute | solution.py:15
  230.0 32.0 %collective-permute-start.11 = (f32[2,4,64,512]{3,2,1,0:T(8,128)S(1)}, f32[2,4,64,512]{3,2,1,0:T(8,128)S(1)}, u32[]{:S(2)}, u32[]{:S(2)}) collective-permute-start(f32[2,4,64,512]{3,2,1,0:T(8,128)S(1)} %get-tuple-element.39), channel_id=1, source_target_pairs={{32,0},{34,2},{36,4},{38,6},{40,8},{42,10},{44,12},{46,14},{48,16}... | collective-permute-start | bytes 3145736 | tf_op jit(solution)/shard_map/ppermute | solution.py:15
  231.3 30.7 %collective-permute-start.10 = (f32[2,4,64,512]{3,2,1,0:T(8,128)S(1)}, f32[2,4,64,512]{3,2,1,0:T(8,128)S(1)}, u32[]{:S(2)}, u32[]{:S(2)}) collective-permute-start(f32[2,4,64,512]{3,2,1,0:T(8,128)S(1)} %get-tuple-element.40), channel_id=1, source_target_pairs={{16,0},{18,2},{20,4},{22,6},{24,8},{26,10},{28,12},{30,14},{32,16}... | collective-permute-start | bytes 3145736 | tf_op jit(solution)/shard_map/ppermute | solution.py:15
  232.6 48.7 %collective-permute-start.9 = (f32[2,4,64,512]{3,2,1,0:T(8,128)S(1)}, f32[2,4,64,512]{3,2,1,0:T(8,128)S(1)}, u32[]{:S(2)}, u32[]{:S(2)}) collective-permute-start(f32[2,4,64,512]{3,2,1,0:T(8,128)S(1)} %get-tuple-element.41), channel_id=1, source_target_pairs={{8,0},{10,2},{12,4},{14,6},{16,8},{18,10},{20,12},{22,14},{24,16},... | collective-permute-start | bytes 3145736 | tf_op jit(solution)/shard_map/ppermute | solution.py:15
  234.1 25.7 %copy-start.2 = (bf16[1,4,640,512]{2,3,1,0:T(8,128)(2,1)S(1)}, bf16[1,4,640,512]{2,3,1,0:T(8,128)(2,1)}, u32[]{:S(2)}) copy-start(bf16[1,4,640,512]{2,3,1,0:T(8,128)(2,1)} %copy-done.1) | copy-start | bytes 7864324
  254.4 47.9 %collective-permute-start.8 = (f32[2,4,64,512]{3,2,1,0:T(8,128)S(1)}, f32[2,4,64,512]{3,2,1,0:T(8,128)S(1)}, u32[]{:S(2)}, u32[]{:S(2)}) collective-permute-start(f32[2,4,64,512]{3,2,1,0:T(8,128)S(1)} %get-tuple-element.42), channel_id=1, source_target_pairs={{4,0},{6,2},{8,4},{10,6},{12,8},{14,10},{16,12},{18,14},{20,16},{2... | collective-permute-start | bytes 3145736 | tf_op jit(solution)/shard_map/ppermute | solution.py:15
  255.7 58.4 %collective-permute-start.7 = (f32[2,4,64,512]{3,2,1,0:T(8,128)S(1)}, f32[2,4,64,512]{3,2,1,0:T(8,128)S(1)}, u32[]{:S(2)}, u32[]{:S(2)}) collective-permute-start(f32[2,4,64,512]{3,2,1,0:T(8,128)S(1)} %fusion.15), channel_id=1, source_target_pairs={{2,0},{4,2},{6,4},{8,6},{10,8},{12,10},{14,12},{16,14},{18,16},{20... | collective-permute-start | bytes 3145736 | tf_op jit(solution)/shard_map/ppermute | solution.py:15
  261.9 54.4 %copy-start.12 = (bf16[2048,512]{1,0:T(8,128)(2,1)S(1)}, bf16[2048,512]{1,0:T(8,128)(2,1)}, u32[]{:S(2)}) copy-start(bf16[2048,512]{1,0:T(8,128)(2,1)} %param.16) | copy-start | bytes 6291460
  319.7 59.1 %copy-start.3 = (bf16[128,2048]{1,0:T(8,128)(2,1)S(1)}, bf16[128,2048]{1,0:T(8,128)(2,1)}, u32[]{:S(2)}) copy-start(bf16[128,2048]{1,0:T(8,128)(2,1)} %param.13) | copy-start | bytes 1572868
  319.7 59.1 %copy-start.19 = (f32[2048]{0:T(1024)S(1)}, f32[2048]{0:T(1024)}, u32[]{:S(2)}) copy-start(f32[2048]{0:T(1024)} %param.14) | copy-start | bytes 24580
  319.7 88.0 %reduce-scatter.3.cloned.1.call-start = ((), (), s32[]{:S(2)}) async-start(), calls=%async_computation.3 | async-start | bytes 1572864 | tf_op jit(solution)/shard_map/reduce_scatter | solution.py:83
  320.0 87.7 %copy-start.15 = (bf16[128,2048]{1,0:T(8,128)(2,1)S(1)}, bf16[128,2048]{1,0:T(8,128)(2,1)}, u32[]{:S(2)}) copy-start(bf16[128,2048]{1,0:T(8,128)(2,1)} %param.19) | copy-start | bytes 1572868
  (7 other events, 13.3 us)
Sparse Core Ops, SparseCore 0:
  10.8 31.6 all-gather.2
  44.3 72.5 all-gather.4
  319.8 58.9 reduce-scatter.4
  381.3 26.3 reduce-scatter.2
where the time goes:
time: 420 us; the launch traced here: 417 us
  waiting for transfers between devices  228 us (54%)
  local copies, waits for them, and re-layouts  91.2 us (22%)
  starting transfers between devices  39.2 us (9%)
  matrix products  25.9 us (6%)
  other arithmetic  17.9 us (4%)
  between operations  14.3 us (3%)
    ppermute x14, waiting for transfers between devices, shifted(): return lax.ppermute(value, axis, pairs)  69.3 us
    reduce_scatter x1, waiting for transfers between devices, per_device(): lax.psum_scatter(grad_normed.astype(jnp.bfloat16), 'tp', scatter_dimensio...  55.4 us
    all_gather x1, waiting for transfers between devices, per_device(): lax.all_gather(out_grad, 'tp', axis=0, tiled=True)  46.3 us
    ppermute x14, starting transfers between devices, shifted(): return lax.ppermute(value, axis, pairs)  39.1 us
    all_gather x1, waiting for transfers between devices, per_device(): lax.all_gather(normed_rows, 'tp', axis=0, tiled=True)  29.2 us
    reduce_scatter x1, waiting for transfers between devices, per_device(): lax.psum_scatter(jnp.dot(mixed_rows, w_out, preferred_element_type=jnp.fl...  27.5 us
    another operation x3, local copies, waits for them, and re-layouts, per_device(): jnp.stack([grad_keys, grad_values])  20.7 us
    unnamed x46, local copies, waits for them, and re-layouts  15.4 us
  transfers between devices with their start and end apart: 18, of which 8 were waited for; matrix products, arithmetic and copies ran while one was open for 11% of the time, Pallas kernels for 0%

commit v1 on v0

--- a/solution.py
+++ b/solution.py
@@ -26,7 +26,9 @@
     normed_rows = (unit_rows * norm_gain).astype(jnp.bfloat16)
     gathered, out_grads = (
         lax.all_gather(normed_rows, "tp", axis=0, tiled=True),
-        lax.all_gather(out_grad, "tp", axis=0, tiled=True),
+        jnp.concatenate(
+            lax.all_to_all(jnp.stack([out_grad] * lax.axis_size("tp")), "tp", 0, 0), axis=0
+        ),
     )
     tokens = gathered.shape[0]
     feat_width = w_query.shape[1]

time: 420 us -> 424 us (level)
  starting transfers between devices: 39.2 us -> 49.4 us
  waiting for transfers between devices: 228 us -> 220 us
    all_gather x1 -> x0, waiting for transfers between devices: 46.3 us -> none  [per_device(): lax.all_gather(out_grad, 'tp', axis=0, tiled=True)]
    reduce_scatter x1, waiting for transfers between devices: 55.4 us -> 81.7 us  [per_device(): lax.psum_scatter(grad_normed.astype(jnp.bfloat16), 'tp', scatter_dimensio...]
    ppermute x14, waiting for transfers between devices: 69.3 us -> 87.9 us  [shifted(): return lax.ppermute(value, axis, pairs)]
    all_gather x1, waiting for transfers between devices: 29.2 us -> 11.5 us  [per_device(): lax.all_gather(normed_rows, 'tp', axis=0, tiled=True)]
    all_to_all x0 -> x1, waiting for transfers between devices: none -> 11.3 us  [per_device(): lax.all_to_all(jnp.stack([out_grad] * lax.axis_size('tp')), 'tp', 0, 0)]
    ppermute x14, starting transfers between devices: 39.1 us -> 44.5 us  [shifted(): return lax.ppermute(value, axis, pairs)]
    all_to_all x0 -> x1, starting transfers between devices: none -> 4.84 us  [per_device(): lax.all_to_all(jnp.stack([out_grad] * lax.axis_size('tp')), 'tp', 0, 0)]
    unnamed x46 -> x42, local copies, waits for them, and re-layouts: 15.4 us -> 15.4 us
  transfers between devices with their start and end apart: 18 -> 18, of which waited for: 8 -> 13; matrix products, arithmetic and copies ran while one was open for 11% -> 11% of each run, Pallas kernels for 0% -> 0%
where the time goes in v1:
time: 424 us; the launch traced here: 421 us
  waiting for transfers between devices  220 us (52%)
  local copies, waits for them, and re-layouts  91.3 us (22%)
  starting transfers between devices  49.4 us (12%)
  matrix products  25.5 us (6%)
  other arithmetic  20.4 us (5%)
  between operations  14.2 us (3%)
    ppermute x14, waiting for transfers between devices, shifted(): return lax.ppermute(value, axis, pairs)  87.9 us
    reduce_scatter x1, waiting for transfers between devices, per_device(): lax.psum_scatter(grad_normed.astype(jnp.bfloat16), 'tp', scatter_dimensio...  81.7 us
    ppermute x14, starting transfers between devices, shifted(): return lax.ppermute(value, axis, pairs)  44.5 us
    reduce_scatter x1, waiting for transfers between devices, per_device(): lax.psum_scatter(jnp.dot(mixed_rows, w_out, preferred_element_type=jnp.fl...  27.7 us
    another operation x3, local copies, waits for them, and re-layouts, per_device(): jnp.stack([grad_keys, grad_values])  20.7 us
    unnamed x42, local copies, waits for them, and re-layouts  15.4 us
    reshape x6, local copies, waits for them, and re-layouts, per_device(): fetched[section].reshape(2, blocks, BLOCK, feat_width)  14.3 us
    concatenate x1, local copies, waits for them, and re-layouts, per_device(): keys_all = jnp.concatenate(pieces, axis=2)  12.3 us
  transfers between devices with their start and end apart: 18, of which 13 were waited for; matrix products, arithmetic and copies ran while one was open for 11% of the time, Pallas kernels for 0%

profile of v1, /device:TPU:1, one launch (start us, length us, event | category | flops | bytes accessed | tf_op | source)
XLA Modules:
  0.0 421.0 jit_solution(7806891646676001152)
XLA Ops:
  13.0 4.8 %all-to-all-start = ((bf16[2,128,2048]{2,1,0:T(8,128)(2,1)}), bf16[2,128,2048]{2,1,0:T(8,128)(2,1)S(1)}, u32[]{:S(2)}, u32[]{:S(2)}) async-start(bf16[2,128,2048]{2,1,0:T(8,128)(2,1)} %pad_maximum_fusion.1), calls=%async_computation.1 | async-start | bytes 2097152 | tf_op jit(solution)/shard_map/all_to_all | solution.py:30
  19.7 11.3 %all-to-all-done = bf16[2,128,2048]{2,1,0:T(8,128)(2,1)S(1)} async-done(((bf16[2,128,2048]{2,1,0:T(8,128)(2,1)}), bf16[2,128,2048]{2,1,0:T(8,128)(2,1)S(1)}, u32[]{:S(2)}, u32[]{:S(2)}) %all-to-all-start) | async-done | bytes 1048608 | tf_op jit(solution)/shard_map/all_to_all | solution.py:30
  33.4 11.5 %all-gather.2.cloned.1.call-done = bf16[256,2048]{1,0:T(8,128)(2,1)} async-done(((bf16[128,2048]{1,0:T(8,128)(2,1)}), bf16[256,2048]{1,0:T(8,128)(2,1)}) %all-gather.2.cloned.1.call-update) | async-done | bytes 1048592 | tf_op jit(solution)/shard_map/all_gather | solution.py:28
  44.9 2.8 convolution_convert_fusion.4
  49.3 3.9 collective-permute-start
  53.2 3.6 collective-permute-start.1
  57.6 6.9 %collective-permute-start.2 = (bf16[2,256,512]{2,1,0:T(8,128)(2,1)}, bf16[2,256,512]{2,1,0:T(8,128)(2,1)}, u32[]{:S(2)}, u32[]{:S(2)}) collective-permute-start(bf16[2,256,512]{2,1,0:T(8,128)(2,1)} %pad_maximum_fusion.2), channel_id=1, source_target_pairs={{0,8},{2,10},{4,12},{6,14},{8,16},{10,18},{12,20},{14,22},{16,24},... | collective-permute-start | bytes 1572872 | tf_op jit(solution)/shard_map/ppermute | solution.py:15
  64.5 3.3 collective-permute-start.3
  67.7 2.7 collective-permute-start.4
  75.2 3.2 collective-permute-start.5
  79.2 8.1 %collective-permute-start.6 = (bf16[2,256,512]{2,1,0:T(8,128)(2,1)}, bf16[2,256,512]{2,1,0:T(8,128)(2,1)}, u32[]{:S(2)}, u32[]{:S(2)}) collective-permute-start(bf16[2,256,512]{2,1,0:T(8,128)(2,1)} %pad_maximum_fusion.2), channel_id=1, source_target_pairs={{0,128},{2,130},{4,132},{6,134},{8,136},{10,138},{12,140},{14,142}... | collective-permute-start | bytes 1572872 | tf_op jit(solution)/shard_map/ppermute | solution.py:15
  109.8 9.8 %collective-permute-done.5 = bf16[2,256,512]{2,1,0:T(8,128)(2,1)} collective-permute-done((bf16[2,256,512]{2,1,0:T(8,128)(2,1)}, bf16[2,256,512]{2,1,0:T(8,128)(2,1)}, u32[]{:S(2)}, u32[]{:S(2)}) %collective-permute-start.5) | collective-permute-done | bytes 524320 | tf_op jit(solution)/shard_map/ppermute | solution.py:15
  122.0 8.9 %collective-permute-done.6 = bf16[2,256,512]{2,1,0:T(8,128)(2,1)} collective-permute-done((bf16[2,256,512]{2,1,0:T(8,128)(2,1)}, bf16[2,256,512]{2,1,0:T(8,128)(2,1)}, u32[]{:S(2)}, u32[]{:S(2)}) %collective-permute-start.6) | collective-permute-done | bytes 524320 | tf_op jit(solution)/shard_map/ppermute | solution.py:15
  133.2 12.3 %concatenate.18 = bf16[2,4,640,512]{2,3,1,0:T(8,128)(2,1)} concatenate(bf16[2,4,64,512]{2,3,1,0:T(8,128)(2,1)S(1)} %pad_maximum_fusion, bf16[2,4,64,512]{2,3,1,0:T(8,128)(2,1)} %copy.64, bf16[2,4,64,512]{2,3,1,0:T(8,128)(2,1)} %copy.65, bf16[2,4,64,512]{2,3,1,0:T(8,128)(2,1)} %copy.66, bf16[2,4,64,512]{2,3,1,0:T(8,128)(2,1)} %copy.27, bf16[2,4,64,512]{2,3,1,0:T(8,128)(2,1)} %copy.28, ...), dimensions={2} | concatenate | bytes 10485760 | tf_op jit(solution)/shard_map/concatenate | solution.py:58
  145.6 3.0 fusion.46
  150.9 3.2 convolution_bitcast_fusion
  156.9 3.3 multiply_bitcast_fusion
  160.2 7.2 %copy.42 = f32[4,640,4,128]{3,2,1,0:T(4,128)} copy(f32[4,640,4,128]{1,3,2,0:T(8,128)} %multiply_bitcast_fusion) | data formatting | bytes 10485760 | tf_op jit(solution)/shard_map/mul | solution.py:107
  167.4 7.4 %stack.39 = f32[1,4,10,64,512]{4,3,2,1,0:T(8,128)} reshape(f32[4,640,4,128]{3,2,1,0:T(4,128)} %copy.42) | data formatting | bytes 10485760 | tf_op jit(solution)/shard_map/stack | solution.py:113
  174.9 5.8 %constant_dynamic-update-slice_fusion.1 = f32[2,4,10,64,512]{4,3,2,1,0:T(8,128)} fusion(f32[1,4,10,64,512]{4,3,2,1,0:T(8,128)} %stack.39), kind=kLoop, calls=%fused_computation.74 | loop fusion | bytes 10485760
  180.7 7.2 %copy.44 = f32[4,640,4,128]{3,2,1,0:T(4,128)} copy(f32[4,640,4,128]{1,3,2,0:T(8,128)} %convolution_bitcast_fusion) | data formatting | bytes 10485760 | tf_op jit(solution)/shard_map/bhqk,bqhe->bkhe/transpose | solution.py:110
  187.9 7.4 %stack.40 = f32[1,4,10,64,512]{4,3,2,1,0:T(8,128)} reshape(f32[4,640,4,128]{3,2,1,0:T(4,128)} %copy.44) | data formatting | bytes 10485760 | tf_op jit(solution)/shard_map/stack | solution.py:113
  195.3 5.9 %constant_dynamic-update-slice_fusion = f32[2,4,10,64,512]{4,3,2,1,0:T(8,128)} fusion(f32[2,4,10,64,512]{4,3,2,1,0:T(8,128)} %constant_dynamic-update-slice_fusion.1, f32[1,4,10,64,512]{4,3,2,1,0:T(8,128)} %stack.40), kind=kLoop, calls=%fused_computation.73 | loop fusion | bytes 10485760 | tf_op jit(solution)/shard_map/stack | solution.py:113
  201.2 4.6 %slice_bitcast_fusion.8 = (f32[2,4,64,512]{3,2,1,0:T(8,128)S(1)}, f32[2,4,64,512]{3,2,1,0:T(8,128)S(1)}, f32[2,4,64,512]{3,2,1,0:T(8,128)S(1)}, f32[2,4,64,512]{...) fusion(f32[2,4,10,64,512]{4,3,2,1,0:T(8,128)} %constant_dynamic, ...), kind=kLoop, calls=%fused_computation.53 | loop fusion | bytes 14680064 | tf_op jit(solution)/shard_map/add | solution.py:116
  215.7 15.6 %collective-permute-done.13 = f32[2,4,64,512]{3,2,1,0:T(8,128)S(1)} collective-permute-done((f32[2,4,64,512]{3,2,1,0:T(8,128)S(1)}, f32[2,4,64,512]{3,2,1,0:T(8,128)S(1)}, u32[]{:S(2)}, u32[]{:S(2)}) %collective-permute-start.13) | collective-permute-done | bytes 1048608 | tf_op jit(solution)/shard_map/ppermute | solution.py:15
  233.3 5.1 %collective-permute-start.7 = (f32[2,4,64,512]{3,2,1,0:T(8,128)S(1)}, f32[2,4,64,512]{3,2,1,0:T(8,128)S(1)}, u32[]{:S(2)}, u32[]{:S(2)}) collective-permute-start(f32[2,4,64,512]{3,2,1,0:T(8,128)S(1)} %fusion.15), channel_id=1, source_target_pairs={{2,0},{4,2},{6,4},{8,6},{10,8},{12,10},{14,12},{16,14},{18,16},{20... | collective-permute-start | bytes 3145736 | tf_op jit(solution)/shard_map/ppermute | solution.py:15
  240.8 35.3 %collective-permute-done.9 = f32[2,4,64,512]{3,2,1,0:T(8,128)S(1)} collective-permute-done((f32[2,4,64,512]{3,2,1,0:T(8,128)S(1)}, f32[2,4,64,512]{3,2,1,0:T(8,128)S(1)}, u32[]{:S(2)}, u32[]{:S(2)}) %collective-permute-start.9) | collective-permute-done | bytes 1048608 | tf_op jit(solution)/shard_map/ppermute | solution.py:15
  276.6 15.1 %collective-permute-done.7 = f32[2,4,64,512]{3,2,1,0:T(8,128)S(1)} collective-permute-done((f32[2,4,64,512]{3,2,1,0:T(8,128)S(1)}, f32[2,4,64,512]{3,2,1,0:T(8,128)S(1)}, u32[]{:S(2)}, u32[]{:S(2)}) %collective-permute-start.7) | collective-permute-done | bytes 1048608 | tf_op jit(solution)/shard_map/ppermute | solution.py:15
  297.6 3.3 convolution_convert_fusion
  301.0 81.7 %reduce-scatter.5.cloned.1.call-done = bf16[128,2048]{1,0:T(8,128)(2,1)} async-done(((bf16[256,2048]{1,0:T(8,128)(2,1)}), bf16[128,2048]{1,0:T(8,128)(2,1)}) %reduce-scatter.5.cloned.1.call-update) | async-done | bytes 524304 | tf_op jit(solution)/shard_map/reduce_scatter | solution.py:133
  384.1 27.7 %reduce-scatter.3.cloned.1.call-done = bf16[128,2048]{1,0:T(8,128)(2,1)} async-done(((bf16[256,2048]{1,0:T(8,128)(2,1)}), bf16[128,2048]{1,0:T(8,128)(2,1)}) %reduce-scatter.3.cloned.1.call-update) | async-done | bytes 524304 | tf_op jit(solution)/shard_map/reduce_scatter | solution.py:85
  411.8 2.7 fusion.12
  (119 shorter events, 72.0 us)
Async XLA Ops:
  7.2 65.3 %copy-start = (bf16[2048,512]{1,0:T(8,128)(2,1)S(1)}, bf16[2048,512]{1,0:T(8,128)(2,1)}, u32[]{:S(2)}) copy-start(bf16[2048,512]{1,0:T(8,128)(2,1)} %param.15) | copy-start | bytes 6291460
  7.2 37.7 %all-gather.2.cloned.1.call-start = ((), (), s32[]{:S(2)}) async-start(), calls=%async_computation.3 | async-start | bytes 1572864 | tf_op jit(solution)/shard_map/all_gather | solution.py:28
  13.0 18.0 %all-to-all-start = ((bf16[2,128,2048]{2,1,0:T(8,128)(2,1)}), bf16[2,128,2048]{2,1,0:T(8,128)(2,1)S(1)}, u32[]{:S(2)}, u32[]{:S(2)}) async-start(bf16[2,128,2048]{2,1,0:T(8,128)(2,1)} %pad_maximum_fusion.1), calls=%async_computation.1 | async-start | bytes 2097152 | tf_op jit(solution)/shard_map/all_to_all | solution.py:30
  17.8 364.9 %reduce-scatter.5.cloned.1.call-start = ((), (), s32[]{:S(2)}) async-start(), calls=%async_computation.5 | async-start | bytes 1572864 | tf_op jit(solution)/shard_map/reduce_scatter | solution.py:133
  33.4 117.5 %copy-start.4 = (bf16[4,64,4,128]{3,2,1,0:T(4,128)(2,1)}, bf16[4,64,4,128]{3,2,1,0:T(4,128)(2,1)S(1)}, u32[]{:S(2)}) copy-start(bf16[4,64,4,128]{3,2,1,0:T(4,128)(2,1)S(1)} %reshape.222) | copy-start | bytes 786436
  44.9 2.8 copy-start.9
  44.9 2.8 copy-start.18
  47.7 22.8 %copy-start.7 = (bf16[256,512]{1,0:T(8,128)(2,1)}, bf16[256,512]{1,0:T(8,128)(2,1)S(1)}, u32[]{:S(2)}) copy-start(bf16[256,512]{1,0:T(8,128)(2,1)S(1)} %convolution_convert_fusion.4) | copy-start | bytes 786436
  48.4 26.0 %copy-start.8 = (bf16[256,512]{1,0:T(8,128)(2,1)}, bf16[256,512]{1,0:T(8,128)(2,1)S(1)}, u32[]{:S(2)}) copy-start(bf16[256,512]{1,0:T(8,128)(2,1)S(1)} %convolution_convert_fusion.5) | copy-start | bytes 786436
  49.3 25.9 %collective-permute-start = (bf16[2,256,512]{2,1,0:T(8,128)(2,1)}, bf16[2,256,512]{2,1,0:T(8,128)(2,1)}, u32[]{:S(2)}, u32[]{:S(2)}) collective-permute-start(bf16[2,256,512]{2,1,0:T(8,128)(2,1)} %pad_maximum_fusion.2), channel_id=1, source_target_pairs={{0,2},{2,4},{4,6},{6,8},{8,10},{10,12},{12,14},{14,16},{16,18},{18... | collective-permute-start | bytes 1572872 | tf_op jit(solution)/shard_map/ppermute | solution.py:15
  53.2 25.2 %collective-permute-start.1 = (bf16[2,256,512]{2,1,0:T(8,128)(2,1)}, bf16[2,256,512]{2,1,0:T(8,128)(2,1)S(1)}, u32[]{:S(2)}, u32[]{:S(2)}) collective-permute-start(bf16[2,256,512]{2,1,0:T(8,128)(2,1)} %pad_maximum_fusion.2), channel_id=1, source_target_pairs={{0,4},{2,6},{4,8},{6,10},{8,12},{10,14},{12,16},{14,18},{16,20},{1... | collective-permute-start | bytes 1572872 | tf_op jit(solution)/shard_map/ppermute | solution.py:15
  57.6 43.2 %collective-permute-start.2 = (bf16[2,256,512]{2,1,0:T(8,128)(2,1)}, bf16[2,256,512]{2,1,0:T(8,128)(2,1)}, u32[]{:S(2)}, u32[]{:S(2)}) collective-permute-start(bf16[2,256,512]{2,1,0:T(8,128)(2,1)} %pad_maximum_fusion.2), channel_id=1, source_target_pairs={{0,8},{2,10},{4,12},{6,14},{8,16},{10,18},{12,20},{14,22},{16,24},... | collective-permute-start | bytes 1572872 | tf_op jit(solution)/shard_map/ppermute | solution.py:15
  64.5 38.8 %collective-permute-start.3 = (bf16[2,256,512]{2,1,0:T(8,128)(2,1)}, bf16[2,256,512]{2,1,0:T(8,128)(2,1)}, u32[]{:S(2)}, u32[]{:S(2)}) collective-permute-start(bf16[2,256,512]{2,1,0:T(8,128)(2,1)} %pad_maximum_fusion.2), channel_id=1, source_target_pairs={{0,16},{2,18},{4,20},{6,22},{8,24},{10,26},{12,28},{14,30},{16,32}... | collective-permute-start | bytes 1572872 | tf_op jit(solution)/shard_map/ppermute | solution.py:15
  67.7 39.7 %collective-permute-start.4 = (bf16[2,256,512]{2,1,0:T(8,128)(2,1)}, bf16[2,256,512]{2,1,0:T(8,128)(2,1)}, u32[]{:S(2)}, u32[]{:S(2)}) collective-permute-start(bf16[2,256,512]{2,1,0:T(8,128)(2,1)} %pad_maximum_fusion.2), channel_id=1, source_target_pairs={{0,32},{2,34},{4,36},{6,38},{8,40},{10,42},{12,44},{14,46},{16,48}... | collective-permute-start | bytes 1572872 | tf_op jit(solution)/shard_map/ppermute | solution.py:15
  75.2 44.4 %collective-permute-start.5 = (bf16[2,256,512]{2,1,0:T(8,128)(2,1)}, bf16[2,256,512]{2,1,0:T(8,128)(2,1)}, u32[]{:S(2)}, u32[]{:S(2)}) collective-permute-start(bf16[2,256,512]{2,1,0:T(8,128)(2,1)} %pad_maximum_fusion.2), channel_id=1, source_target_pairs={{0,64},{2,66},{4,68},{6,70},{8,72},{10,74},{12,76},{14,78},{16,80}... | collective-permute-start | bytes 1572872 | tf_op jit(solution)/shard_map/ppermute | solution.py:15
  79.2 51.6 %collective-permute-start.6 = (bf16[2,256,512]{2,1,0:T(8,128)(2,1)}, bf16[2,256,512]{2,1,0:T(8,128)(2,1)}, u32[]{:S(2)}, u32[]{:S(2)}) collective-permute-start(bf16[2,256,512]{2,1,0:T(8,128)(2,1)} %pad_maximum_fusion.2), channel_id=1, source_target_pairs={{0,128},{2,130},{4,132},{6,134},{8,136},{10,138},{12,140},{14,142}... | collective-permute-start | bytes 1572872 | tf_op jit(solution)/shard_map/ppermute | solution.py:15
  145.6 3.1 copy-start.6
  145.6 3.1 copy-start.15
  150.9 3.3 copy-start.11
  205.8 25.5 %collective-permute-start.13 = (f32[2,4,64,512]{3,2,1,0:T(8,128)S(1)}, f32[2,4,64,512]{3,2,1,0:T(8,128)S(1)}, u32[]{:S(2)}, u32[]{:S(2)}) collective-permute-start(f32[2,4,64,512]{3,2,1,0:T(8,128)S(1)} %get-tuple-element.43), channel_id=1, source_target_pairs={{128,0},{130,2},{132,4},{134,6},{136,8},{138,10},{140,12},{142,14}... | collective-permute-start | bytes 3145736 | tf_op jit(solution)/shard_map/ppermute | solution.py:15
  207.1 26.1 %collective-permute-start.12 = (f32[2,4,64,512]{3,2,1,0:T(8,128)S(1)}, f32[2,4,64,512]{3,2,1,0:T(8,128)S(1)}, u32[]{:S(2)}, u32[]{:S(2)}) collective-permute-start(f32[2,4,64,512]{3,2,1,0:T(8,128)S(1)} %get-tuple-element.44), channel_id=1, source_target_pairs={{64,0},{66,2},{68,4},{70,6},{72,8},{74,10},{76,12},{78,14},{80,16}... | collective-permute-start | bytes 3145736 | tf_op jit(solution)/shard_map/ppermute | solution.py:15
  208.4 32.1 %collective-permute-start.11 = (f32[2,4,64,512]{3,2,1,0:T(8,128)S(1)}, f32[2,4,64,512]{3,2,1,0:T(8,128)S(1)}, u32[]{:S(2)}, u32[]{:S(2)}) collective-permute-start(f32[2,4,64,512]{3,2,1,0:T(8,128)S(1)} %get-tuple-element.39), channel_id=1, source_target_pairs={{32,0},{34,2},{36,4},{38,6},{40,8},{42,10},{44,12},{46,14},{48,16}... | collective-permute-start | bytes 3145736 | tf_op jit(solution)/shard_map/ppermute | solution.py:15
  209.7 31.0 %collective-permute-start.10 = (f32[2,4,64,512]{3,2,1,0:T(8,128)S(1)}, f32[2,4,64,512]{3,2,1,0:T(8,128)S(1)}, u32[]{:S(2)}, u32[]{:S(2)}) collective-permute-start(f32[2,4,64,512]{3,2,1,0:T(8,128)S(1)} %get-tuple-element.40), channel_id=1, source_target_pairs={{16,0},{18,2},{20,4},{22,6},{24,8},{26,10},{28,12},{30,14},{32,16}... | collective-permute-start | bytes 3145736 | tf_op jit(solution)/shard_map/ppermute | solution.py:15
  211.0 65.0 %collective-permute-start.9 = (f32[2,4,64,512]{3,2,1,0:T(8,128)S(1)}, f32[2,4,64,512]{3,2,1,0:T(8,128)S(1)}, u32[]{:S(2)}, u32[]{:S(2)}) collective-permute-start(f32[2,4,64,512]{3,2,1,0:T(8,128)S(1)} %get-tuple-element.41), channel_id=1, source_target_pairs={{8,0},{10,2},{12,4},{14,6},{16,8},{18,10},{20,12},{22,14},{24,16},... | collective-permute-start | bytes 3145736 | tf_op jit(solution)/shard_map/ppermute | solution.py:15
  212.6 25.8 %copy-start.2 = (bf16[1,4,640,512]{2,3,1,0:T(8,128)(2,1)S(1)}, bf16[1,4,640,512]{2,3,1,0:T(8,128)(2,1)}, u32[]{:S(2)}) copy-start(bf16[1,4,640,512]{2,3,1,0:T(8,128)(2,1)} %copy-done.1) | copy-start | bytes 7864324
  231.3 45.3 %collective-permute-start.8 = (f32[2,4,64,512]{3,2,1,0:T(8,128)S(1)}, f32[2,4,64,512]{3,2,1,0:T(8,128)S(1)}, u32[]{:S(2)}, u32[]{:S(2)}) collective-permute-start(f32[2,4,64,512]{3,2,1,0:T(8,128)S(1)} %get-tuple-element.42), channel_id=1, source_target_pairs={{4,0},{6,2},{8,4},{10,6},{12,8},{14,10},{16,12},{18,14},{20,16},{2... | collective-permute-start | bytes 3145736 | tf_op jit(solution)/shard_map/ppermute | solution.py:15
  233.3 58.4 %collective-permute-start.7 = (f32[2,4,64,512]{3,2,1,0:T(8,128)S(1)}, f32[2,4,64,512]{3,2,1,0:T(8,128)S(1)}, u32[]{:S(2)}, u32[]{:S(2)}) collective-permute-start(f32[2,4,64,512]{3,2,1,0:T(8,128)S(1)} %fusion.15), channel_id=1, source_target_pairs={{2,0},{4,2},{6,4},{8,6},{10,8},{12,10},{14,12},{16,14},{18,16},{20... | collective-permute-start | bytes 3145736 | tf_op jit(solution)/shard_map/ppermute | solution.py:15
  240.5 53.4 %copy-start.10 = (bf16[2048,512]{1,0:T(8,128)(2,1)S(1)}, bf16[2048,512]{1,0:T(8,128)(2,1)}, u32[]{:S(2)}) copy-start(bf16[2048,512]{1,0:T(8,128)(2,1)} %param.16) | copy-start | bytes 6291460
  297.3 85.4 %copy-start.3 = (bf16[128,2048]{1,0:T(8,128)(2,1)S(1)}, bf16[128,2048]{1,0:T(8,128)(2,1)}, u32[]{:S(2)}) copy-start(bf16[128,2048]{1,0:T(8,128)(2,1)} %param.13) | copy-start | bytes 1572868
  297.3 85.4 %copy-start.17 = (f32[2048]{0:T(1024)S(1)}, f32[2048]{0:T(1024)}, u32[]{:S(2)}) copy-start(f32[2048]{0:T(1024)} %param.14) | copy-start | bytes 24580
  297.3 114.4 %reduce-scatter.3.cloned.1.call-start = ((), (), s32[]{:S(2)}) async-start(), calls=%async_computation.4 | async-start | bytes 1572864 | tf_op jit(solution)/shard_map/reduce_scatter | solution.py:85
  297.6 114.2 %copy-start.13 = (bf16[128,2048]{1,0:T(8,128)(2,1)S(1)}, bf16[128,2048]{1,0:T(8,128)(2,1)}, u32[]{:S(2)}) copy-start(bf16[128,2048]{1,0:T(8,128)(2,1)} %param.19) | copy-start | bytes 1572868
  (5 other events, 7.7 us)
Sparse Core Ops, SparseCore 0:
  10.8 34.0 all-gather.1
  297.4 85.2 reduce-scatter.4
  385.4 26.3 reduce-scatter.2
